TPU v7x, 256 devices: a whole 4x4x8 slice. The times are simulated.
256 devices in a mesh: slab: 64 (over x, z, core), img: 4 (over y).
Axes of the slice: x: 4, y: 4, z: 8, core: 2. Of those that a mesh axis runs over, the one named last changes fastest.
Arguments:
- volume: bfloat16 [32768, 256], P('slab'), may hold values from -6 to 6
- interp: bfloat16 [4, 64, 16, 32768], P('img', None, None, 'slab'), may hold values from -0.09375 to 0.09375
- block_index: int32 [4, 64, 64], P('img'), may hold values from 0 to 7
- images: bfloat16 [4, 1024, 128, 256], P('img', 'slab'), may hold values from -6 to 6
- defocus: float32 [4, 1024], P('img', 'slab'), may hold values from 5000 to 25000
- orient: int32 [4, 1024, 4], P('img', 'slab'), may hold values from 0 to 63, all different within a row
Outputs:
- update: float32 [32768, 256], P('slab')
- weights: float32 [4, 1024, 64], P('img', 'slab')
Inputs may be any that keep to these rules, and one draw needn't show every extreme that they name: `orient`: each image lists 4 different orientations of its group.
All inputs are finite; a program needn't handle non-finite values.
Results may differ from a plain program's by a relative error of at most 0.0077.
Values may be sent and summed in bfloat16 or wider, within the bound.
A program may use at most 64 MiB of HBM per device.

v0:
```python
import math
import jax
import jax.numpy as jnp
from jax import lax
from jax.sharding import PartitionSpec as P

BOX = 256
NS = 16
wave_length = 0.0197
aberration = 27000000.0
amplitude = 0.1
grid_side = 4


def phase_tables(fourier, shifts, box):
    freq = (jnp.arange(fourier, dtype=jnp.int32) - fourier // 2).astype(jnp.float32)
    shift_steps = jnp.arange(shifts, dtype=jnp.int32)
    shift_x = (2 * (shift_steps // grid_side) - (grid_side - 1)).astype(jnp.float32)
    shift_y = (2 * (shift_steps % grid_side) - (grid_side - 1)).astype(jnp.float32)
    angle = 2.0 * math.pi / box * (freq[:, None, None] * shift_x + freq[None, :, None] * shift_y)
    forward = jnp.stack([jnp.cos(angle), jnp.sin(angle)], axis=1).reshape(
        2 * fourier * fourier, shifts
    )
    backward = jnp.stack([jnp.cos(angle), -jnp.sin(angle)], axis=1).reshape(
        2 * fourier * fourier, shifts
    )
    return (forward.astype(jnp.bfloat16), backward.T.astype(jnp.bfloat16))


def contrast(defocus_blk, fourier, box):
    freq = (jnp.arange(fourier, dtype=jnp.int32) - fourier // 2).astype(jnp.float32)
    wave_sq = (freq[:, None] * freq[:, None] + freq[None, :] * freq[None, :]) / (box * box)
    phase = math.pi * wave_length * defocus_blk[:, None, None] * wave_sq
    phase = phase - 0.5 * math.pi * aberration * wave_length**3 * wave_sq * wave_sq
    return -(math.sqrt(1.0 - amplitude * amplitude) * jnp.sin(phase) + amplitude * jnp.cos(phase))


def correlate(panels, image_blk, list_blk, defocus_blk, phase_fwd, phase_back, box):
    count = image_blk.shape[0]
    fourier = image_blk.shape[1]
    picks = list_blk.shape[1]
    shifts = phase_fwd.shape[1]
    ctf = contrast(defocus_blk, fourier, box)
    weighted = ctf[:, :, None, :] * image_blk.astype(jnp.float32).reshape(
        count, fourier, 2, fourier
    )
    real_u = weighted[:, None, :, 0]
    imag_u = weighted[:, None, :, 1]
    chosen = panels[list_blk].astype(jnp.float32).reshape(count, picks, fourier, 2, fourier)
    real_p = chosen[:, :, :, 0]
    imag_p = chosen[:, :, :, 1]
    product = jnp.stack(
        [real_p * real_u + imag_p * imag_u, real_p * imag_u - imag_p * real_u], axis=3
    )
    product = product.astype(jnp.bfloat16).reshape(count * picks, 2 * fourier * fourier)
    scores = jnp.dot(product, phase_fwd, preferred_element_type=jnp.float32) / fourier
    scores = scores.reshape(count, picks * shifts)
    squared = scores * scores
    weights = squared / (jnp.mean(squared, axis=1, keepdims=True) + 1e-05)
    rounded = weights.astype(jnp.bfloat16).reshape(count * picks, shifts)
    spread = jnp.dot(rounded, phase_back, preferred_element_type=jnp.float32)
    spread = spread.reshape(count, picks, fourier, 2, fourier)
    real_e = spread[:, :, :, 0]
    imag_e = spread[:, :, :, 1]
    backed = jnp.stack(
        [real_u * real_e - imag_u * imag_e, real_u * imag_e + imag_u * real_e], axis=3
    )
    backed = backed.astype(jnp.bfloat16).reshape(count * picks, 2 * fourier * fourier)
    return (weights, backed)


def on_device(volume, interp, block_index, images, defocus, orient):
    slab_count = lax.axis_size("slab")
    slab_index = lax.axis_index("slab")
    orient_count = interp.shape[1]
    ori_dev = orient_count // slab_count
    block_rows = interp.shape[2]
    fourier = images.shape[2]
    block_count = fourier // block_rows
    img_dev = images.shape[1]
    picks = orient.shape[2]
    levels = jnp.arange(block_count, dtype=jnp.int32)
    partial_value = jnp.einsum("jpr,rx->jpx", interp[0], volume, preferred_element_type=jnp.float32)
    owned_idx = lax.dynamic_slice_in_dim(block_index[0], slab_index * ori_dev, ori_dev, 0)
    received = lax.all_to_all(
        partial_value.reshape(slab_count, ori_dev * block_rows, 2 * fourier),
        "slab",
        split_axis=0,
        concat_axis=0,
        tiled=True,
    ).reshape(slab_count, ori_dev, block_rows, 2 * fourier)
    place = (owned_idx[:, :, None] == levels).astype(jnp.float32)
    summed = jnp.einsum(
        "osb,sopx->obpx",
        place,
        received,
        precision=lax.Precision.HIGHEST,
        preferred_element_type=jnp.float32,
    ).reshape(ori_dev, fourier, 2 * fourier)
    panels = lax.all_gather(summed.astype(jnp.bfloat16), "slab", axis=0, tiled=True)
    phase_fwd, phase_back = phase_tables(fourier, NS, BOX)
    blk = math.gcd(img_dev, 32)
    blk_total = img_dev // blk

    def per_block(pieces):
        image_blk, list_blk, defocus_blk = pieces
        return correlate(panels, image_blk, list_blk, defocus_blk, phase_fwd, phase_back, BOX)

    weights, backs = lax.map(
        per_block,
        (
            images[0].reshape(blk_total, blk, fourier, 2 * fourier),
            orient[0].reshape(blk_total, blk, picks),
            defocus[0].reshape(blk_total, blk),
        ),
    )
    all_slices = backs.reshape(img_dev * picks, 2 * fourier * fourier)
    member = (
        orient[0].reshape(-1)[:, None] == jnp.arange(orient_count, dtype=jnp.int32)[None, :]
    ).astype(jnp.bfloat16)
    contrib = lax.dot_general(
        member, all_slices, (((0,), (0,)), ((), ())), preferred_element_type=jnp.float32
    ).reshape(orient_count, fourier, 2 * fourier)
    gathered = lax.all_to_all(
        contrib.astype(jnp.bfloat16), "slab", split_axis=0, concat_axis=0, tiled=True
    ).reshape(slab_count, ori_dev, fourier, 2 * fourier)
    back_own = jnp.sum(gathered.astype(jnp.float32), axis=0).astype(jnp.bfloat16)
    back_own = back_own.reshape(ori_dev, block_count, block_rows, 2 * fourier)
    chosen_back = (owned_idx[:, :, None] == levels).astype(jnp.bfloat16)
    outgoing = jnp.einsum(
        "osb,obpx->sopx", chosen_back, back_own, preferred_element_type=jnp.float32
    )
    outgoing = outgoing.astype(jnp.bfloat16).reshape(slab_count * ori_dev, block_rows, 2 * fourier)
    incoming = lax.all_to_all(outgoing, "slab", split_axis=0, concat_axis=0, tiled=True)
    column = jnp.einsum("jpr,jpx->rx", interp[0], incoming, preferred_element_type=jnp.float32)
    summed_cols = lax.psum(column, "img")
    update = summed_cols / math.sqrt(img_dev * slab_count)
    return (update, weights)


def solution(mesh):
    return jax.shard_map(
        on_device,
        mesh=mesh,
        in_specs=(
            P("slab", None),
            P("img", None, None, "slab"),
            P("img", None, None),
            P("img", "slab", None, None),
            P("img", "slab"),
            P("img", "slab", None),
        ),
        out_specs=(P("slab", None), P("img", "slab", None)),
        check_vma=False,
    )
```

profile of v0, /device:TPU:2, one launch (start us, length us, event | category | flops | bytes accessed | tf_op | source)
XLA Modules:
  0.0 393.0 jit_solution(16889548143787505688)
XLA Ops:
  8.4 2.4 fusion.13
  10.8 12.0 %all-to-all-start = ((f32[64,16,256]{2,1,0:T(8,128)}), f32[64,16,256]{2,1,0:T(8,128)S(1)}, u32[]{:S(2)}, u32[]{:S(2)}) async-start(f32[64,16,256]{2,1,0:T(8,128)} %fusion.13), calls=%async_computation | async-start | bytes 2097152 | tf_op jit(solution)/shard_map/all_to_all | solution.py:85
  23.5 26.4 %all-to-all-done = f32[64,16,256]{2,1,0:T(8,128)S(1)} async-done(((f32[64,16,256]{2,1,0:T(8,128)}), f32[64,16,256]{2,1,0:T(8,128)S(1)}, u32[]{:S(2)}, u32[]{:S(2)}) %all-to-all-start) | async-done | bytes 1048608 | tf_op jit(solution)/shard_map/all_to_all | solution.py:85
  54.4 5.4 %fusion.17 = (bf16[128,1,128,16]{2,3,1,0:T(8,128)(2,1)S(1)}, bf16[128,1,128,16]{2,3,1,0:T(8,128)(2,1)}, bf16[128,1,128,16]{2,3,1,0:T(8,128)(2,1)S(1)}) fusion(f32[128,16]{0,1:T(8,128)S(1)} %get-tuple-element.51, f32[128,16]{1,0:T(8,128)S(1)} %copy.67), kind=kLoop, calls=%fused_computation.33 | loop fusion | flops 1572864 | bytes 1589248 | tf_op jit(solution)/shard_map/convert.8
  62.6 2.6 convert_element_type.150
  65.4 3.9 add_negate_fusion
  71.7 56.5 %all-gather.2.cloned.1.call-done = bf16[64,128,256]{2,1,0:T(8,128)(2,1)} async-done(((bf16[1,128,256]{2,1,0:T(8,128)(2,1)}), bf16[64,128,256]{2,1,0:T(8,128)(2,1)}) %all-gather.2.cloned.1.call-update) | async-done | bytes 4194320 | tf_op jit(solution)/shard_map/all_gather | solution.py:100
  128.2 5.0 %gather_fusion = bf16[64,128,256]{2,1,0:T(8,128)(2,1)} fusion(bf16[64,128,256]{2,1,0:T(8,128)(2,1)} %all-gather.2.cloned.1.call-done, s32[1024]{0:T(1024)S(1)} %pad_clamp_fusion), kind=kCustom, calls=%fused_computation | custom fusion | bytes 8388864 | tf_op jit(solution)/shard_map/while/body/eval_jaxpr/gather | solution.py:49
  133.1 7.0 %copy.63 = f32[64,128,256]{1,2,0:T(8,128)} copy(bf16[64,128,256]{2,1,0:T(8,128)(2,1)} %gather_fusion) | data formatting | bytes 12582912 | tf_op jit(solution)/shard_map/while/body/eval_jaxpr/convert_element_type | solution.py:49
  140.1 7.8 %fusion.39 = (f32[16,4,128,1,128]{2,4,3,1,0:T(8,128)}, f32[16,4,128,1,128]{2,4,3,1,0:T(8,128)}) fusion(f32[16,4,128,2,128]{2,4,3,1,0:T(8,128)} %bitcast.64), kind=kLoop, calls=%fused_computation.74 | loop fusion | bytes 16777216 | tf_op jit(solution)/shard_map/while/body/eval_jaxpr/slice | solution.py:50
  147.9 5.5 %copy.83 = f32[16,4,128,1,128]{4,0,3,2,1:T(8,128)} copy(f32[16,4,128,1,128]{2,4,3,1,0:T(8,128)} %get-tuple-element.41) | data formatting | bytes 8388608
  153.4 5.5 %copy.84 = f32[16,4,128,1,128]{4,0,3,2,1:T(8,128)} copy(f32[16,4,128,1,128]{2,4,3,1,0:T(8,128)} %get-tuple-element.42) | data formatting | bytes 8388608
  158.9 4.9 %add_convert_fusion.1 = (bf16[16,4,128,1,128]{4,0,3,2,1:T(8,128)(2,1)S(1)}, bf16[16,4,128,1,128]{4,0,3,2,1:T(8,128)(2,1)S(1)}) fusion(f32[16,4,128,1,128]{4,0,3,2,1:T(8,128)} %copy.84, f32[16,4,128,1,128]{4,0,3,2,1:T(8,128)} %copy.83, f32[16,128,128]{2,0,1:T(8,128)} %get-tuple-element.44, f32[16,128,128]{2,0,1:T(8,128)S(1)} %get-tuple-element.43), kind=kLoop, calls=%fused_computation.9 | loop fusion | flops 8388608 | bytes 14680064 | tf_op jit(solution)/shard_map/convert.9
  164.2 6.6 %copy.66 = bf16[16,4,128,2,128]{4,3,2,1,0:T(2,128)(2,1)} copy(bf16[16,4,128,2,128]{4,0,3,2,1:T(8,128)(2,1)S(1)} %pad_maximum_fusion) | data formatting | bytes 8388608 | tf_op jit(solution)/shard_map/while/body/eval_jaxpr/stack | solution.py:52
  170.8 7.8 %convert_element_type.147 = bf16[64,32768]{1,0:T(8,128)(2,1)} reshape(bf16[16,4,128,2,128]{4,3,2,1,0:T(2,128)(2,1)} %copy.66) | data formatting | bytes 8388608 | tf_op jit(solution)/shard_map/while/body/eval_jaxpr/convert_element_type | solution.py:55
  178.6 3.7 fusion.40
  187.1 6.6 %copy.71 = bf16[16,4,128,2,128]{4,3,2,1,0:T(2,128)(2,1)} copy(bf16[16,4,128,2,128]{4,0,3,2,1:T(8,128)(2,1)S(1)} %pad_maximum_fusion.1) | data formatting | bytes 8388608 | tf_op jit(solution)/shard_map/while/body/eval_jaxpr/stack | solution.py:65
  193.7 7.9 %convert_element_type.152 = bf16[64,32768]{1,0:T(8,128)(2,1)} reshape(bf16[16,4,128,2,128]{4,3,2,1,0:T(2,128)(2,1)} %copy.71) | data formatting | bytes 8388608 | tf_op jit(solution)/shard_map/while/body/eval_jaxpr/convert_element_type | solution.py:68
  201.5 3.4 fusion.3
  204.9 2.4 copy.73
  207.4 102.1 %all_to_all.15 = bf16[64,128,256]{2,1,0:T(8,128)(2,1)} all-to-all(bf16[64,128,256]{2,1,0:T(8,128)(2,1)S(1)} %copy.73), channel_id=1, replica_groups=mesh['slab'=64,'img'=4] {'slab'}, dimensions={0} | all-to-all | bytes 8388608 | tf_op jit(solution)/shard_map/all_to_all | solution.py:124
  309.4 2.8 reduce_sum.32
  312.9 24.0 %all_to_all.16 = bf16[64,16,256]{2,1,0:T(8,128)(2,1)S(1)} all-to-all(bf16[64,16,256]{2,1,0:T(8,128)(2,1)S(1)} %copy.75), channel_id=1, replica_groups=mesh['slab'=64,'img'=4] {'slab'}, dimensions={0} | all-to-all | bytes 1048576 | tf_op jit(solution)/shard_map/all_to_all | solution.py:134
  339.0 45.1 %all-reduce.2.cloned.1.call-done = f32[512,256]{0,1:T(8,128)} async-done(((f32[512,256]{0,1:T(8,128)}), f32[512,256]{0,1:T(8,128)}) %all-reduce.2.cloned.1.call-update) | async-done | bytes 524304 | tf_op jit(solution)/shard_map/psum | solution.py:136
  (56 shorter events, 21.7 us)
Async XLA Ops:
  7.2 1.2 copy-start
  7.2 44.7 %copy-start.4 = (s32[1,16,4]{1,2,0:T(4,128)S(1)}, s32[1,16,4]{1,2,0:T(4,128)}, u32[]{:S(2)}) copy-start(s32[1,16,4]{1,2,0:T(4,128)} %param.11) | copy-start | bytes 772
  10.8 39.2 %all-to-all-start = ((f32[64,16,256]{2,1,0:T(8,128)}), f32[64,16,256]{2,1,0:T(8,128)S(1)}, u32[]{:S(2)}, u32[]{:S(2)}) async-start(f32[64,16,256]{2,1,0:T(8,128)} %fusion.13), calls=%async_computation | async-start | bytes 2097152 | tf_op jit(solution)/shard_map/all_to_all | solution.py:85
  22.8 105.4 %all-gather.2.cloned.1.call-start = ((), (), s32[]{:S(2)}) async-start(), calls=%async_computation.3 | async-start | bytes 4259840 | tf_op jit(solution)/shard_map/all_gather | solution.py:100
  51.6 332.5 %all-reduce.2.cloned.1.call-start = ((), (), s32[]{:S(2)}) async-start(), calls=%async_computation.4 | async-start | bytes 1048576 | tf_op jit(solution)/shard_map/psum | solution.py:136
  54.2 11.1 %copy-start.5 = (f32[1,16]{1,0:T(1,128)S(1)}, f32[1,16]{1,0:T(1,128)}, u32[]{:S(2)}) copy-start(f32[1,16]{1,0:T(1,128)} %param.10) | copy-start | bytes 196
  59.8 0.8 copy-start.2
  178.6 4.3 %copy-start.3 = (bf16[128,1,128,16]{2,3,1,0:T(8,128)(2,1)S(1)}, bf16[128,1,128,16]{2,3,1,0:T(8,128)(2,1)}, u32[]{:S(2)}) copy-start(bf16[128,1,128,16]{2,3,1,0:T(8,128)(2,1)} %copy-done.2) | copy-start | bytes 1572868
  182.8 2.4 copy-start.1
Sparse Core Ops, SparseCore 0:
  51.7 76.3 all-gather.1
  338.3 45.7 all-reduce.1
where the time goes:
time: 394 us; the launch traced here: 393 us
  waiting for transfers between devices  128 us (32%)
  blocking collectives  126 us (32%)
  local copies, waits for them, and re-layouts  75.3 us (19%)
  other arithmetic  22.6 us (6%)
  matrix products  14.5 us (4%)
  between operations  14.3 us (4%)
  starting transfers between devices  12.3 us (3%)
    all_to_all x1, blocking collectives, on_device(): lax.all_to_all(contrib.astype(jnp.bfloat16), 'slab', split_axis=0, concat...  102 us
    all_gather x1, waiting for transfers between devices, on_device(): lax.all_gather(summed.astype(jnp.bfloat16), 'slab', axis=0, tiled=True)  56.5 us
    psum x1, waiting for transfers between devices, on_device(): summed_cols = lax.psum(column, 'img')  45.1 us
    all_to_all x1, waiting for transfers between devices, on_device(): lax.all_to_all(partial_value.reshape(slab_count, ori_dev * block_rows, 2...  26.4 us
    all_to_all x1, blocking collectives, on_device(): lax.all_to_all(outgoing, 'slab', split_axis=0, concat_axis=0, tiled=True)  24 us
    unnamed x16, local copies, waits for them, and re-layouts  14.1 us
    all_to_all x1, starting transfers between devices, on_device(): lax.all_to_all(partial_value.reshape(slab_count, ori_dev * block_rows, 2...  12 us
    another operation x3, other arithmetic  11.8 us
  transfers between devices with their start and end apart: 3, of which 3 were waited for; matrix products, arithmetic and copies ran while one was open for 5% of the time, Pallas kernels for 0%

commit v1 on v0

--- a/solution.py
+++ b/solution.py
@@ -1,3 +1,4 @@
+import functools
 import math
 import jax
 import jax.numpy as jnp
@@ -10,6 +11,15 @@
 aberration = 27000000.0
 amplitude = 0.1
 grid_side = 4
+
+
+def track_keys(point, mesh_name, dim_k):
+    val = jnp.stack([point for _ in range(lax.psum(1, axis_name=mesh_name))], axis=0)
+    near = lax.all_to_all(val, axis_name=mesh_name, split_axis=0, concat_axis=0)
+    return jnp.concatenate(near, axis=dim_k)
+
+
+prepare_loops = functools.partial(track_keys, mesh_name="slab", dim_k=0)
 
 
 def phase_tables(fourier, shifts, box):
@@ -97,7 +107,7 @@
         precision=lax.Precision.HIGHEST,
         preferred_element_type=jnp.float32,
     ).reshape(ori_dev, fourier, 2 * fourier)
-    panels = lax.all_gather(summed.astype(jnp.bfloat16), "slab", axis=0, tiled=True)
+    panels = prepare_loops(summed.astype(jnp.bfloat16))
     phase_fwd, phase_back = phase_tables(fourier, NS, BOX)
     blk = math.gcd(img_dev, 32)
     blk_total = img_dev // blk

time: 394 us -> 422 us (1.071)
  waiting for transfers between devices: 128 us -> 146 us
  starting transfers between devices: 12.3 us -> 20.2 us
    all_to_all x0 -> x1, waiting for transfers between devices: none -> 74.7 us  [track_keys(): near = lax.all_to_all(val, axis_name=mesh_name, split_axis=0, concat_axis=0)]
    all_gather x1 -> x0, waiting for transfers between devices: 56.5 us -> none  [on_device(): lax.all_gather(summed.astype(jnp.bfloat16), 'slab', axis=0, tiled=True)]
    all_to_all x0 -> x1, starting transfers between devices: none -> 7.94 us  [track_keys(): near = lax.all_to_all(val, axis_name=mesh_name, split_axis=0, concat_axis=0)]
where the time goes in v1:
time: 422 us; the launch traced here: 420 us
  waiting for transfers between devices  146 us (35%)
  blocking collectives  125 us (30%)
  local copies, waits for them, and re-layouts  77.3 us (18%)
  other arithmetic  22.6 us (5%)
  starting transfers between devices  20.2 us (5%)
  matrix products  14.5 us (3%)
  between operations  14.3 us (3%)
    all_to_all x1, blocking collectives, on_device(): lax.all_to_all(contrib.astype(jnp.bfloat16), 'slab', split_axis=0, concat...  101 us
    all_to_all x1, waiting for transfers between devices, track_keys(): near = lax.all_to_all(val, axis_name=mesh_name, split_axis=0, concat_axis=0)  74.7 us
    psum x1, waiting for transfers between devices, on_device(): summed_cols = lax.psum(column, 'img')  45.3 us
    all_to_all x1, waiting for transfers between devices, on_device(): lax.all_to_all(partial_value.reshape(slab_count, ori_dev * block_rows, 2...  26.4 us
    all_to_all x1, blocking collectives, on_device(): lax.all_to_all(outgoing, 'slab', split_axis=0, concat_axis=0, tiled=True)  24 us
    unnamed x16, local copies, waits for them, and re-layouts  14.1 us
    all_to_all x1, starting transfers between devices, on_device(): lax.all_to_all(partial_value.reshape(slab_count, ori_dev * block_rows, 2...  12 us
    another operation x3, other arithmetic  11.8 us
  transfers between devices with their start and end apart: 3, of which 3 were waited for; matrix products, arithmetic and copies ran while one was open for 5% of the time, Pallas kernels for 0%

profile of v1, /device:TPU:2, one launch (start us, length us, event | category | flops | bytes accessed | tf_op | source)
XLA Modules:
  0.0 420.4 jit_solution(12538484572159524902)
XLA Ops:
  10.8 12.0 %all-to-all-start = ((f32[64,16,256]{2,1,0:T(8,128)}), f32[64,16,256]{2,1,0:T(8,128)S(1)}, u32[]{:S(2)}, u32[]{:S(2)}) async-start(f32[64,16,256]{2,1,0:T(8,128)} %fusion.13), calls=%async_computation | async-start | bytes 2097152 | tf_op jit(solution)/shard_map/all_to_all | solution.py:95
  23.5 26.4 %all-to-all-done = f32[64,16,256]{2,1,0:T(8,128)S(1)} async-done(((f32[64,16,256]{2,1,0:T(8,128)}), f32[64,16,256]{2,1,0:T(8,128)S(1)}, u32[]{:S(2)}, u32[]{:S(2)}) %all-to-all-start) | async-done | bytes 1048608 | tf_op jit(solution)/shard_map/all_to_all | solution.py:95
  51.0 2.5 stack.20
  53.5 7.9 %all-to-all-start.1 = ((bf16[64,1,128,256]{3,2,1,0:T(8,128)(2,1)}), bf16[64,1,128,256]{3,2,1,0:T(8,128)(2,1)}, u32[]{:S(2)}, u32[]{:S(2)}) async-start(bf16[64,1,128,256]{3,2,1,0:T(8,128)(2,1)} %stack.20), calls=%async_computation.1 | async-start | bytes 8388608 | tf_op jit(solution)/shard_map/all_to_all | solution.py:18
  64.2 5.4 %fusion.17 = (bf16[128,1,128,16]{2,3,1,0:T(8,128)(2,1)S(1)}, bf16[128,1,128,16]{2,3,1,0:T(8,128)(2,1)}, bf16[128,1,128,16]{2,3,1,0:T(8,128)(2,1)S(1)}) fusion(f32[128,16]{0,1:T(8,128)S(1)} %get-tuple-element.51, f32[128,16]{1,0:T(8,128)S(1)} %copy.62), kind=kLoop, calls=%fused_computation.33 | loop fusion | flops 1572864 | bytes 1589248 | tf_op jit(solution)/shard_map/convert.8
  72.5 2.6 convert_element_type.149
  75.3 3.9 add_negate_fusion
  81.6 74.7 %all-to-all-done.1 = bf16[64,1,128,256]{3,2,1,0:T(8,128)(2,1)} async-done(((bf16[64,1,128,256]{3,2,1,0:T(8,128)(2,1)}), bf16[64,1,128,256]{3,2,1,0:T(8,128)(2,1)}, u32[]{:S(2)}, u32[]{:S(2)}) %all-to-all-start.1) | async-done | bytes 4194336 | tf_op jit(solution)/shard_map/all_to_all | solution.py:18
  156.3 5.0 %gather_fusion = bf16[64,128,256]{2,1,0:T(8,128)(2,1)} fusion(bf16[64,128,256]{2,1,0:T(8,128)(2,1)} %bitcast.8, s32[1024]{0:T(1024)S(1)} %pad_clamp_fusion), kind=kCustom, calls=%fused_computation | custom fusion | bytes 8388864 | tf_op jit(solution)/shard_map/while/body/eval_jaxpr/gather | solution.py:59
  161.2 7.0 %copy.58 = f32[64,128,256]{1,2,0:T(8,128)} copy(bf16[64,128,256]{2,1,0:T(8,128)(2,1)} %gather_fusion) | data formatting | bytes 12582912 | tf_op jit(solution)/shard_map/while/body/eval_jaxpr/convert_element_type | solution.py:59
  168.2 7.8 %fusion.39 = (f32[16,4,128,1,128]{2,4,3,1,0:T(8,128)}, f32[16,4,128,1,128]{2,4,3,1,0:T(8,128)}) fusion(f32[16,4,128,2,128]{2,4,3,1,0:T(8,128)} %bitcast.65), kind=kLoop, calls=%fused_computation.74 | loop fusion | bytes 16777216 | tf_op jit(solution)/shard_map/while/body/eval_jaxpr/slice | solution.py:60
  176.0 5.5 %copy.82 = f32[16,4,128,1,128]{4,0,3,2,1:T(8,128)} copy(f32[16,4,128,1,128]{2,4,3,1,0:T(8,128)} %get-tuple-element.41) | data formatting | bytes 8388608
  181.5 5.5 %copy.83 = f32[16,4,128,1,128]{4,0,3,2,1:T(8,128)} copy(f32[16,4,128,1,128]{2,4,3,1,0:T(8,128)} %get-tuple-element.42) | data formatting | bytes 8388608
  187.0 4.9 %add_convert_fusion.1 = (bf16[16,4,128,1,128]{4,0,3,2,1:T(8,128)(2,1)S(1)}, bf16[16,4,128,1,128]{4,0,3,2,1:T(8,128)(2,1)S(1)}) fusion(f32[16,4,128,1,128]{4,0,3,2,1:T(8,128)} %copy.83, f32[16,4,128,1,128]{4,0,3,2,1:T(8,128)} %copy.82, f32[16,128,128]{2,0,1:T(8,128)} %get-tuple-element.44, f32[16,128,128]{2,0,1:T(8,128)S(1)} %get-tuple-element.43), kind=kLoop, calls=%fused_computation.9 | loop fusion | flops 8388608 | bytes 14680064 | tf_op jit(solution)/shard_map/convert.9
  192.3 6.6 %copy.61 = bf16[16,4,128,2,128]{4,3,2,1,0:T(2,128)(2,1)} copy(bf16[16,4,128,2,128]{4,0,3,2,1:T(8,128)(2,1)S(1)} %pad_maximum_fusion) | data formatting | bytes 8388608 | tf_op jit(solution)/shard_map/while/body/eval_jaxpr/stack | solution.py:62
  198.9 7.8 %convert_element_type.146 = bf16[64,32768]{1,0:T(8,128)(2,1)} reshape(bf16[16,4,128,2,128]{4,3,2,1,0:T(2,128)(2,1)} %copy.61) | data formatting | bytes 8388608 | tf_op jit(solution)/shard_map/while/body/eval_jaxpr/convert_element_type | solution.py:65
  206.7 3.7 fusion.40
  215.2 6.6 %copy.66 = bf16[16,4,128,2,128]{4,3,2,1,0:T(2,128)(2,1)} copy(bf16[16,4,128,2,128]{4,0,3,2,1:T(8,128)(2,1)S(1)} %pad_maximum_fusion.1) | data formatting | bytes 8388608 | tf_op jit(solution)/shard_map/while/body/eval_jaxpr/stack | solution.py:75
  221.8 7.9 %convert_element_type.151 = bf16[64,32768]{1,0:T(8,128)(2,1)} reshape(bf16[16,4,128,2,128]{4,3,2,1,0:T(2,128)(2,1)} %copy.66) | data formatting | bytes 8388608 | tf_op jit(solution)/shard_map/while/body/eval_jaxpr/convert_element_type | solution.py:78
  229.6 3.4 fusion.3
  235.5 101.2 %all_to_all.20 = bf16[64,128,256]{2,1,0:T(8,128)(2,1)} all-to-all(bf16[64,128,256]{2,1,0:T(8,128)(2,1)S(1)} %copy.68), channel_id=1, replica_groups=mesh['slab'=64,'img'=4] {'slab'}, dimensions={0} | all-to-all | bytes 8388608 | tf_op jit(solution)/shard_map/all_to_all | solution.py:134
  336.6 2.8 reduce_sum.32
  340.1 24.0 %all_to_all.21 = bf16[64,16,256]{2,1,0:T(8,128)(2,1)S(1)} all-to-all(bf16[64,16,256]{2,1,0:T(8,128)(2,1)S(1)} %copy.70), channel_id=1, replica_groups=mesh['slab'=64,'img'=4] {'slab'}, dimensions={0} | all-to-all | bytes 1048576 | tf_op jit(solution)/shard_map/all_to_all | solution.py:144
  366.2 45.3 %all-reduce.2.cloned.1.call-done = f32[512,256]{0,1:T(8,128)} async-done(((f32[512,256]{0,1:T(8,128)}), f32[512,256]{0,1:T(8,128)}) %all-reduce.2.cloned.1.call-update) | async-done | bytes 524304 | tf_op jit(solution)/shard_map/psum | solution.py:146
  (56 shorter events, 25.9 us)
Async XLA Ops:
  7.2 1.2 copy-start
  10.8 39.2 %all-to-all-start = ((f32[64,16,256]{2,1,0:T(8,128)}), f32[64,16,256]{2,1,0:T(8,128)S(1)}, u32[]{:S(2)}, u32[]{:S(2)}) async-start(f32[64,16,256]{2,1,0:T(8,128)} %fusion.13), calls=%async_computation | async-start | bytes 2097152 | tf_op jit(solution)/shard_map/all_to_all | solution.py:95
  53.5 8.2 %copy-start.4 = (s32[1,16,4]{1,2,0:T(4,128)S(1)}, s32[1,16,4]{1,2,0:T(4,128)}, u32[]{:S(2)}) copy-start(s32[1,16,4]{1,2,0:T(4,128)} %param.11) | copy-start | bytes 772
  53.5 102.8 %all-to-all-start.1 = ((bf16[64,1,128,256]{3,2,1,0:T(8,128)(2,1)}), bf16[64,1,128,256]{3,2,1,0:T(8,128)(2,1)}, u32[]{:S(2)}, u32[]{:S(2)}) async-start(bf16[64,1,128,256]{3,2,1,0:T(8,128)(2,1)} %stack.20), calls=%async_computation.1 | async-start | bytes 8388608 | tf_op jit(solution)/shard_map/all_to_all | solution.py:18
  61.4 350.1 %all-reduce.2.cloned.1.call-start = ((), (), s32[]{:S(2)}) async-start(), calls=%async_computation.4 | async-start | bytes 1048576 | tf_op jit(solution)/shard_map/psum | solution.py:146
  64.0 11.2 %copy-start.5 = (f32[1,16]{1,0:T(1,128)S(1)}, f32[1,16]{1,0:T(1,128)}, u32[]{:S(2)}) copy-start(f32[1,16]{1,0:T(1,128)} %param.10) | copy-start | bytes 196
  69.6 0.8 copy-start.2
  206.7 4.3 %copy-start.3 = (bf16[128,1,128,16]{2,3,1,0:T(8,128)(2,1)S(1)}, bf16[128,1,128,16]{2,3,1,0:T(8,128)(2,1)}, u32[]{:S(2)}) copy-start(bf16[128,1,128,16]{2,3,1,0:T(8,128)(2,1)} %copy-done.2) | copy-start | bytes 1572868
  210.9 2.4 copy-start.1
Sparse Core Ops, SparseCore 0:
  365.5 45.9 all-reduce.1
